TPU v7x, 32 devices: a whole 2x2x4 slice. The times are simulated.
32 devices in a mesh: req: 2 (over x), ctx: 4 (over y, core), tp: 4 (over z).
Axes of the slice: x: 2, y: 2, z: 4, core: 2. Of those that a mesh axis runs over, the one named last changes fastest.
Arguments:
- queries: bfloat16 [512, 16, 128], P('req', 'tp'), may hold values from -5 to 5
- new_keys: bfloat16 [512, 4, 128], P('req', 'tp'), may hold values from -5 to 5
- new_values: bfloat16 [512, 4, 128], P('req', 'tp'), may hold values from -24 to 24
- cache_keys: bfloat16 [2, 8192, 4, 128], P('req', 'ctx', 'tp'), may hold values from -5 to 5
- cache_values: bfloat16 [2, 8192, 4, 128], P('req', 'ctx', 'tp'), may hold values from -24 to 24
- cache_lengths: int32 [2], replicated, may hold values from 1 to 8192, as said below
- residual: bfloat16 [512, 2048], P(('req', 'ctx'), 'tp'), may hold values from -24 to 24
- out_weight: bfloat16 [2048, 2048], P('tp', 'ctx'), may hold values from -0.52734375 to 0.52734375
- norm_gain: float32 [2048], replicated, may hold values from 0.1 to 1.9
- expert_ids: int32 [512, 6], P(('req', 'ctx')), may hold values from 0 to 63, all different within a row; in each aligned block of 64 rows (0 to 63, 64 to 127, ...) at most 8 rows name the same one
- gate_weights: float32 [512, 6], P(('req', 'ctx')), may hold values from 0.1 to 1
- w_gate: bfloat16 [64, 2048, 1408], P('req', 'ctx', 'tp'), may hold values from -0.125 to 0.125
- w_up: bfloat16 [64, 2048, 1408], P('req', 'ctx', 'tp'), may hold values from -0.125 to 0.125
- w_down: bfloat16 [64, 1408, 2048], P('req', 'tp', 'ctx'), may hold values from -0.15625 to 0.15625
Outputs:
- layer_out: bfloat16 [512, 2048], P(('req', 'ctx'), 'tp')
Inputs may be any that keep to these rules, and one draw needn't show every extreme that they name: `cache_lengths`: the longest cached length equals 8192. `expert_ids`: within each aligned block of 64 tokens no expert is named by more than 8 routes, a bound that some block reaches.
All inputs are finite; a program needn't handle non-finite values.
Results may differ from a plain program's by a relative error of at most 0.006.
Values may be sent and summed in bfloat16 or wider, within the bound.
A program may use at most 384 MiB of HBM per device.

v0:
```python
import jax
import jax.numpy as jnp
from jax import lax
from jax.sharding import PartitionSpec as P

HD = 128
TOP = 6
CAP = 8
masked_score = -1e30


def merged_2(value, axis, join):
    pieces = jax.tree.map(lambda part: lax.all_gather(part, axis), value)
    head = jax.tree.map(lambda part: part[0], pieces)
    tail = jax.tree.map(lambda part: part[1:], pieces)
    so_far, _ = lax.scan(lambda so_far, piece: (join(so_far, piece), None), head, tail)
    return so_far


def joined_outputs(left_part, right_portion):
    highest = jnp.maximum(left_part[0], right_portion[0])
    left_factor = jnp.exp(left_part[0] - highest)
    right_factor = jnp.exp(right_portion[0] - highest)
    totals = left_part[1] * left_factor + right_portion[1] * right_factor
    numerator = left_part[2] * left_factor[..., None] + right_portion[2] * right_factor[..., None]
    return (highest, totals, numerator)


def body(
    queries,
    new_keys,
    new_values,
    cache_keys,
    cache_values,
    cache_lengths,
    residual,
    out_weight,
    norm_gain,
    expert_ids,
    gate_weights,
    w_gate,
    w_up,
    w_down,
):
    ctx_pos = lax.axis_index("ctx")
    tp_pos = lax.axis_index("tp")
    req_pos = lax.axis_index("req")
    ctx_count = lax.axis_size("ctx")
    tp_count = lax.axis_size("tp")
    req_count = lax.axis_size("req")
    tok_dev, head_count, head_size = queries.shape
    cache_dev = cache_keys.shape[1]
    model_width = w_down.shape[2] * ctx_count
    d_share = residual.shape[1]
    expert_mixture_device = tok_dev // ctx_count
    scale = 1.0 / HD**0.5
    query_flat = queries.reshape(tok_dev * head_count, head_size)
    key_rows = jnp.concatenate([cache_keys[0, :, 0, :], new_keys[:, 0, :]], 0)
    value_rows = jnp.concatenate([cache_values[0, :, 0, :], new_values[:, 0, :]], 0)
    length = lax.dynamic_index_in_dim(cache_lengths, req_pos, 0, keepdims=False)
    cache_valid = ctx_pos * cache_dev + jnp.arange(cache_dev, dtype=jnp.int32) < length
    is_last = ctx_pos == ctx_count - 1
    positions = jnp.arange(tok_dev, dtype=jnp.int32)
    causal = jnp.logical_and(positions[None, :] <= positions[:, None], is_last)
    valid = jnp.concatenate(
        [jnp.broadcast_to(cache_valid[None, :], (tok_dev, cache_dev)), causal], 1
    )
    scores = jnp.dot(query_flat, key_rows.T, preferred_element_type=jnp.float32) * scale
    scores = scores.reshape(tok_dev, head_count, cache_dev + tok_dev)
    scores = jnp.where(valid[:, None, :], scores, masked_score)
    local_max = jnp.max(scores, -1)
    probabilities = jnp.where(valid[:, None, :], jnp.exp(scores - local_max[..., None]), 0.0)
    local_sum = jnp.sum(probabilities, -1)
    rounded = probabilities.astype(jnp.bfloat16)
    numerator = jnp.einsum("thk,kd->thd", rounded, value_rows, preferred_element_type=jnp.float32)
    row_start = ctx_pos * expert_mixture_device
    col_start = tp_pos * d_share
    highest, totals, merged = merged_2((local_max, local_sum, numerator), "ctx", joined_outputs)
    attention_result = merged / totals[..., None]
    attention_result = lax.dynamic_slice_in_dim(
        attention_result, row_start, expert_mixture_device, 0
    )
    attention_result = attention_result.astype(jnp.bfloat16).reshape(
        expert_mixture_device, head_count * head_size
    )
    partial_value = jnp.dot(
        attention_result,
        lax.all_gather(out_weight, "ctx", axis=1, tiled=True),
        preferred_element_type=jnp.float32,
    )
    corner = lax.dynamic_slice_in_dim(partial_value, col_start, d_share, 1) + residual.astype(
        jnp.float32
    )
    partial_value = lax.dynamic_update_slice(partial_value, corner, (jnp.int32(0), col_start))
    hidden = lax.psum(partial_value, "tp")
    mean_square = jnp.mean(hidden * hidden, -1, keepdims=True)
    normed = (hidden * lax.rsqrt(mean_square + 1e-06) * norm_gain).astype(jnp.bfloat16)
    full_gate, full_up, full_down = (
        lax.all_gather(w_gate, "ctx", axis=1, tiled=True),
        lax.all_gather(w_up, "ctx", axis=1, tiled=True),
        lax.all_gather(w_down, "ctx", axis=2, tiled=True),
    )
    exp_dev = w_gate.shape[0]
    experts_all = exp_dev * req_count
    flat_ids = expert_ids.reshape(-1)
    route_count = flat_ids.shape[0]
    matches = (flat_ids[:, None] == jnp.arange(experts_all, dtype=jnp.int32)[None, :]).astype(
        jnp.int32
    )
    rank_in = jnp.sum(jnp.cumsum(matches, 0) * matches, 1) - 1
    slot_index = flat_ids * CAP + rank_in
    source = jnp.arange(route_count, dtype=jnp.int32) // TOP
    outgoing = (
        jnp.zeros((experts_all * CAP, model_width), jnp.bfloat16).at[slot_index].set(normed[source])
    )
    outgoing = outgoing.reshape(req_count, exp_dev, CAP, model_width)
    gathered = lax.all_to_all(outgoing, "req", split_axis=0, concat_axis=0, tiled=True)
    gate_act = jnp.einsum("resd,edf->resf", gathered, full_gate, preferred_element_type=jnp.float32)
    up_act = jnp.einsum("resd,edf->resf", gathered, full_up, preferred_element_type=jnp.float32)
    inner = (jax.nn.silu(gate_act) * up_act).astype(jnp.bfloat16)
    down_act = jnp.einsum("resf,efd->resd", inner, full_down, preferred_element_type=jnp.float32)
    expert_out = down_act.astype(jnp.bfloat16)
    returned_rows = lax.all_to_all(
        lax.all_to_all(expert_out, "req", split_axis=0, concat_axis=0, tiled=True),
        "tp",
        split_axis=3,
        concat_axis=2,
        tiled=True,
    )
    slot_sums = (
        returned_rows.reshape(req_count, exp_dev, tp_count, CAP, d_share).astype(jnp.float32).sum(2)
    )
    slot_sums = slot_sums.reshape(experts_all * CAP, d_share)
    picked = slot_sums[slot_index] * gate_weights.reshape(-1)[:, None]
    expert_mixture = picked.reshape(expert_mixture_device, TOP, d_share).sum(1)
    residual_part = lax.dynamic_slice_in_dim(hidden, col_start, d_share, 1)
    return (residual_part + expert_mixture).astype(jnp.bfloat16)


def solution(mesh):
    in_specs = (
        P("req", "tp", None),
        P("req", "tp", None),
        P("req", "tp", None),
        P("req", "ctx", "tp", None),
        P("req", "ctx", "tp", None),
        P(),
        P(("req", "ctx"), "tp"),
        P("tp", "ctx"),
        P(),
        P(("req", "ctx"), None),
        P(("req", "ctx"), None),
        P("req", "ctx", "tp"),
        P("req", "ctx", "tp"),
        P("req", "tp", "ctx"),
    )
    out_specs = P(("req", "ctx"), "tp")
    return jax.shard_map(body, mesh=mesh, in_specs=in_specs, out_specs=out_specs, check_vma=False)
```

profile of v0, /device:TPU:0, one launch (start us, length us, event | category | flops | bytes accessed | tf_op | source)
XLA Modules:
  0.0 1105.6 jit_solution(16539856928096114020)
XLA Ops:
  6.6 1.3 dynamic_slice.24
  7.9 0.7 add_compare_fusion
  8.5 0.2 pad_add_fusion
  8.7 3.5 broadcast_in_dim.48.clone
  12.2 5.6 broadcast_in_dim.49
  17.8 6.7 fusion.14
  24.7 11.4 %reshape.151 = f32[256,4,2304]{2,1,0:T(4,128)} reshape(f32[1024,2304]{1,0:T(8,128)} %get-tuple-element.92) | data formatting | bytes 18874368 | tf_op jit(solution)/shard_map/reshape | solution.py:69
  36.1 8.0 fusion.15
  44.2 0.7 all-gather.7.cloned.1.call-update
  45.0 0.1 all_gather.30
  45.1 5.3 select_reduce_fusion
  50.4 0.1 all_gather.32
  50.6 6.2 all_gather.33
  56.9 5.9 all_gather.31
  62.8 6.9 all-gather.15.cloned.1.call-done
  69.7 1.1 slice.40
  70.8 0.3 copy.69
  71.1 1.1 slice-done
  72.2 4.9 while.14
  72.2 0.1 copy.128
  72.4 0.1 copy.129
  72.5 1.3 fusion.75
  73.9 0.1 copy.128
  74.0 0.2 copy.129
  74.2 1.3 fusion.75
  75.5 0.1 copy.128
  75.7 0.1 copy.129
  75.9 1.3 fusion.75
  77.2 0.1 copy.71
  77.3 0.1 fusion.55
  77.5 16.4 %all-gather.7.cloned.1.call-done = bf16[512,2048]{1,0:T(8,128)(2,1)} async-done(((bf16[512,512]{1,0:T(8,128)(2,1)}), bf16[512,2048]{1,0:T(8,128)(2,1)}) %all-gather.7.cloned.1.call-update) | async-done | bytes 2097168 | tf_op jit(solution)/shard_map/all_gather | solution.py:88
  93.9 2.1 fusion.59
  96.0 0.8 copy-done.2
  96.9 0.5 all-gather.9.cloned.1.call-update
  97.5 0.5 all-gather.11.cloned.1.call-update
  98.1 0.5 all-gather.13.cloned.1.call-update
  98.8 0.1 eq.33
  98.9 0.1 eq.29
  99.1 0.9 reduce-window.6
  100.0 0.2 slice_reduce_fusion
  100.4 0.1 mul.102
  100.7 34.6 %all-reduce.2.cloned.1.call-done = f32[64,2048]{1,0:T(8,128)} async-done(((f32[64,2048]{1,0:T(8,128)}), f32[64,2048]{1,0:T(8,128)}) %all-reduce.2.cloned.1.call-update) | async-done | bytes 524304 | tf_op jit(solution)/shard_map/psum | solution.py:95
  135.3 1.2 multiply_reduce_fusion.1
  136.5 1.2 multiply_convert_fusion
  137.7 9.7 scatter_custom_fusion
  147.3 28.3 %all_to_all.19 = bf16[2,32,8,2048]{3,2,1,0:T(8,128)(2,1)S(1)} all-to-all(bf16[2,32,8,2048]{3,2,1,0:T(8,128)(2,1)} %bitcast.108), channel_id=1, replica_groups=mesh['req'=2,'ctx'=4,'tp'=4] {'req'}, dimensions={0} | all-to-all | bytes 4194304 | tf_op jit(solution)/shard_map/all_to_all | solution.py:117
  175.6 234.8 %all-gather.9.cloned.1.call-done = bf16[32,2048,352]{1,2,0:T(8,128)(2,1)} async-done(((bf16[32,512,352]{1,2,0:T(8,128)(2,1)}), bf16[32,2048,352]{1,2,0:T(8,128)(2,1)}) %all-gather.9.cloned.1.call-update) | async-done | bytes 46137360 | tf_op jit(solution)/shard_map/all_gather | solution.py:99
  410.4 24.8 %fusion.28 = f32[2,32,8,352]{3,2,0,1:T(8,128)S(1)} fusion(bf16[32,2048,352]{1,2,0:T(8,128)(2,1)} %all-gather.9.cloned.1.call-done, bf16[2,32,8,2048]{3,2,1,0:T(8,128)(2,1)S(1)} %all_to_all.19), kind=kOutput, calls=%fused_computation.38 | convolution fusion | flops 738197504 | bytes 48955392 | tf_op jit(solution)/shard_map/resd,edf->resf/dot_general | solution.py:118
  435.1 250.3 %all-gather.11.cloned.1.call-done = bf16[32,2048,352]{1,2,0:T(8,128)(2,1)} async-done(((bf16[32,512,352]{1,2,0:T(8,128)(2,1)}), bf16[32,2048,352]{1,2,0:T(8,128)(2,1)}) %all-gather.11.cloned.1.call-update) | async-done | bytes 46137360 | tf_op jit(solution)/shard_map/all_gather | solution.py:100
  685.4 25.0 %fusion.43 = bf16[2,32,8,352]{3,2,0,1:T(8,128)(2,1)S(1)} fusion(bf16[32,2048,352]{1,2,0:T(8,128)(2,1)} %all-gather.11.cloned.1.call-done, bf16[2,32,8,2048]{3,2,1,0:T(8,128)(2,1)S(1)} %all_to_all.19, f32[2,32,8,352]{3,2,0,1:T(8,128)S(1)} %fusion.28), kind=kOutput, calls=%fused_computation.41 | convolution fusion | flops 739278848 | bytes 49315840 | tf_op jit(solution)/shard_map/resd,edf->resf/dot_general | solution.py:119
  710.5 250.0 %all-gather.13.cloned.1.call-done = bf16[32,352,2048]{2,1,0:T(8,128)(2,1)} async-done(((bf16[32,352,512]{2,1,0:T(8,128)(2,1)}), bf16[32,352,2048]{2,1,0:T(8,128)(2,1)}) %all-gather.13.cloned.1.call-update) | async-done | bytes 46137360 | tf_op jit(solution)/shard_map/all_gather | solution.py:101
  960.5 17.5 %fusion.21 = bf16[2,32,8,2048]{3,2,0,1:T(8,128)(2,1)S(1)} fusion(bf16[2,32,8,352]{3,2,0,1:T(8,128)(2,1)S(1)} %fusion.43, bf16[32,352,2048]{2,1,0:T(8,128)(2,1)} %all-gather.13.cloned.1.call-done), kind=kOutput, calls=%fused_computation.32 | convolution fusion | flops 739246080 | bytes 48594944 | tf_op jit(solution)/shard_map/resf,efd->resd/dot_general | solution.py:121
  978.0 0.1 copy.78
  978.1 28.1 %all_to_all.20 = bf16[2,32,8,2048]{3,2,1,0:T(8,128)(2,1)S(1)} all-to-all(bf16[2,32,8,2048]{3,2,1,0:T(8,128)(2,1)S(1)} %copy.78), channel_id=1, replica_groups=mesh['req'=2,'ctx'=4,'tp'=4] {'req'}, dimensions={0} | all-to-all | bytes 4194304 | tf_op jit(solution)/shard_map/all_to_all | solution.py:124
  1006.2 9.1 copy.79
  1015.3 10.5 reshape.199
  1025.8 4.9 all-to-all-start.2
  1030.9 47.7 %all-to-all-done.2 = bf16[4,2,131072]{2,1,0:T(2,128)(2,1)S(1)} async-done(((bf16[4,2,131072]{2,1,0:T(2,128)(2,1)}), bf16[4,2,131072]{2,1,0:T(2,128)(2,1)S(1)}, u32[]{:S(2)}, u32[]{:S(2)}) %all-to-all-start.2) | async-done | bytes 2097184 | tf_op jit(solution)/shard_map/all_to_all | solution.py:123
  1078.5 5.6 reshape.200
  1084.1 7.5 convert_reduce_fusion
  1091.6 3.2 copy.81
  1094.9 1.6 gather_fusion
  1096.6 0.4 multiply_reduce_fusion
  1097.0 1.6 add_convert_fusion
  (57 shorter events, 1.6 us)
Async XLA Ops:
  6.5 11.3 %copy-start = (bf16[256,4,128]{2,1,0:T(4,128)(2,1)S(1)}, bf16[256,4,128]{2,1,0:T(4,128)(2,1)}, u32[]{:S(2)}) copy-start(bf16[256,4,128]{2,1,0:T(4,128)(2,1)} %param.16) | copy-start | bytes 786436
  6.5 63.2 %all-gather.15.cloned.1.call-start = ((), (), s32[]{:S(2)}) async-start(), calls=%async_computation.8 | async-start | bytes 2621440 | tf_op jit(solution)/shard_map/all_gather | solution.py:13
  12.2 5.6 copy-start.3
  24.7 11.4 %copy-start.8 = (bf16[256,1,128]{2,0,1:T(8,128)(2,1)S(1)}, bf16[256,1,128]{2,0,1:T(8,128)(2,1)}, u32[]{:S(2)}) copy-start(bf16[256,1,128]{2,0,1:T(8,128)(2,1)} %param.18) | copy-start | bytes 196612
  44.2 49.8 %all-gather.7.cloned.1.call-start = ((), (), s32[]{:S(2)}) async-start(), calls=%async_computation.3 | async-start | bytes 2621440 | tf_op jit(solution)/shard_map/all_gather | solution.py:88
  44.9 90.4 %all-reduce.2.cloned.1.call-start = ((), (), s32[]{:S(2)}) async-start(), calls=%async_computation.4 | async-start | bytes 1048576 | tf_op jit(solution)/shard_map/psum | solution.py:95
  70.8 1.4 slice-start
  77.1 18.8 %copy-start.4 = (bf16[64,512]{1,0:T(8,128)(2,1)S(1)}, bf16[64,512]{1,0:T(8,128)(2,1)}, u32[]{:S(2)}) copy-start(bf16[64,512]{1,0:T(8,128)(2,1)} %param.22) | copy-start | bytes 196612
  96.0 0.8 copy-start.2
  96.8 313.5 %all-gather.9.cloned.1.call-start = ((), (), s32[]{:S(2)}) async-start(), calls=%async_computation.5 | async-start | bytes 57671680 | tf_op jit(solution)/shard_map/all_gather | solution.py:99
  97.4 588.0 %all-gather.11.cloned.1.call-start = ((), (), s32[]{:S(2)}) async-start(), calls=%async_computation.6 | async-start | bytes 57671680 | tf_op jit(solution)/shard_map/all_gather | solution.py:100
  98.0 0.7 copy-start.5
  98.0 38.5 %copy-start.6 = (f32[2048]{0:T(1024)S(1)}, f32[2048]{0:T(1024)}, u32[]{:S(2)}) copy-start(f32[2048]{0:T(1024)} %param.24) | copy-start | bytes 24580
  98.0 862.5 %all-gather.13.cloned.1.call-start = ((), (), s32[]{:S(2)}) async-start(), calls=%async_computation.7 | async-start | bytes 57671680 | tf_op jit(solution)/shard_map/all_gather | solution.py:101
  1025.8 5.0 copy-start.7
  1025.8 52.7 %all-to-all-start.2 = ((bf16[4,2,131072]{2,1,0:T(2,128)(2,1)}), bf16[4,2,131072]{2,1,0:T(2,128)(2,1)S(1)}, u32[]{:S(2)}, u32[]{:S(2)}) async-start(bf16[4,2,131072]{2,1,0:T(2,128)(2,1)} %reshape.199), calls=%async_computation.2 | async-start | bytes 4194304 | tf_op jit(solution)/shard_map/all_to_all | solution.py:123
  1094.9 3.7 copy-start.1
Sparse Core Ops, SparseCore 0:
  44.3 25.3 all-gather.14
  71.3 22.6 all-gather.6
  97.0 38.2 all-reduce.1
  136.7 273.5 all-gather.8
  411.8 273.5 all-gather.10
  686.9 273.5 all-gather.12
where the time goes:
time: 1110 us
  waiting for transfers between devices  843 us (76%)
  matrix products  84 us (8%)
  blocking collectives  68.4 us (6%)
  local copies, waits for them, and re-layouts  67.8 us (6%)
  other arithmetic  23.1 us (2%)
  between operations  14 us (1%)
    all_gather x1, waiting for transfers between devices, body(): lax.all_gather(w_up, 'ctx', axis=1, tiled=True)  250 us
    all_gather x1, waiting for transfers between devices, body(): lax.all_gather(w_down, 'ctx', axis=2, tiled=True)  250 us
    all_gather x1, waiting for transfers between devices, body(): lax.all_gather(w_gate, 'ctx', axis=1, tiled=True)  235 us
    all_to_all x1, waiting for transfers between devices, body(): lax.all_to_all(lax.all_to_all(expert_out, 'req', split_axis=0, concat_axi...  47.7 us
    psum x1, waiting for transfers between devices, body(): hidden = lax.psum(partial_value, 'tp')  34.6 us
    all_to_all x1, blocking collectives, body(): lax.all_to_all(outgoing, 'req', split_axis=0, concat_axis=0, tiled=True)  28.3 us
    all_to_all x1, blocking collectives, body(): lax.all_to_all(expert_out, 'req', split_axis=0, concat_axis=0, tiled=True)  28.1 us
    dot_general x1, matrix products, body(): jnp.einsum('resd,edf->resf', gathered, full_up, preferred_element_type=jn...  25 us
  transfers between devices with their start and end apart: 7, of which 7 were waited for; matrix products, arithmetic and copies ran while one was open for 7% of the time, Pallas kernels for 0%

commit v1 on v0

--- a/solution.py
+++ b/solution.py
@@ -7,6 +7,12 @@
 TOP = 6
 CAP = 8
 masked_score = -1e30
+
+
+def stacked_exchange(value, mesh_axis, split, join):
+    parts = jnp.split(value, lax.axis_size(mesh_axis), axis=split)
+    received = lax.all_to_all(jnp.stack(parts), mesh_axis, 0, 0)
+    return jnp.concatenate(received, axis=join)
 
 
 def merged_2(value, axis, join):
@@ -120,12 +126,8 @@
     inner = (jax.nn.silu(gate_act) * up_act).astype(jnp.bfloat16)
     down_act = jnp.einsum("resf,efd->resd", inner, full_down, preferred_element_type=jnp.float32)
     expert_out = down_act.astype(jnp.bfloat16)
-    returned_rows = lax.all_to_all(
-        lax.all_to_all(expert_out, "req", split_axis=0, concat_axis=0, tiled=True),
-        "tp",
-        split_axis=3,
-        concat_axis=2,
-        tiled=True,
+    returned_rows = stacked_exchange(
+        lax.all_to_all(expert_out, "req", split_axis=0, concat_axis=0, tiled=True), "tp", 3, 2
     )
     slot_sums = (
         returned_rows.reshape(req_count, exp_dev, tp_count, CAP, d_share).astype(jnp.float32).sum(2)

time: 1110 us -> 1070 us (0.964)
  local copies, waits for them, and re-layouts: 67.8 us -> 39.5 us
    unnamed x22 -> x20, local copies, waits for them, and re-layouts: 17.2 us -> 1.1 us
where the time goes in v1:
time: 1070 us
  waiting for transfers between devices  843 us (79%)
  matrix products  84 us (8%)
  blocking collectives  68.2 us (6%)
  local copies, waits for them, and re-layouts  39.5 us (4%)
  other arithmetic  17.5 us (2%)
  between operations  13.8 us (1%)
    all_gather x1, waiting for transfers between devices, body(): lax.all_gather(w_up, 'ctx', axis=1, tiled=True)  250 us
    all_gather x1, waiting for transfers between devices, body(): lax.all_gather(w_down, 'ctx', axis=2, tiled=True)  250 us
    all_gather x1, waiting for transfers between devices, body(): lax.all_gather(w_gate, 'ctx', axis=1, tiled=True)  235 us
    all_to_all x1, waiting for transfers between devices, stacked_exchange(): received = lax.all_to_all(jnp.stack(parts), mesh_axis, 0, 0)  47.7 us
    psum x1, waiting for transfers between devices, body(): hidden = lax.psum(partial_value, 'tp')  34.6 us
    all_to_all x1, blocking collectives, body(): lax.all_to_all(outgoing, 'req', split_axis=0, concat_axis=0, tiled=True)  28.3 us
    all_to_all x1, blocking collectives, body(): lax.all_to_all(expert_out, 'req', split_axis=0, concat_axis=0, tiled=True)  28.1 us
    dot_general x1, matrix products, body(): jnp.einsum('resd,edf->resf', gathered, full_up, preferred_element_type=jn...  25 us
  transfers between devices with their start and end apart: 7, of which 7 were waited for; matrix products, arithmetic and copies ran while one was open for 7% of the time, Pallas kernels for 0%

profile of v1, /device:TPU:0, one launch (start us, length us, event | category | flops | bytes accessed | tf_op | source)
XLA Modules:
  0.0 1071.4 jit_solution(12354337486215563970)
XLA Ops:
  6.6 1.3 dynamic_slice.24
  7.9 0.7 add_compare_fusion
  8.5 0.2 pad_add_fusion
  8.7 3.5 broadcast_in_dim.48.clone
  12.2 5.6 broadcast_in_dim.49
  17.8 6.7 fusion.14
  24.5 0.1 sub.35
  24.7 11.4 %reshape.148 = f32[256,4,2304]{2,1,0:T(4,128)} reshape(f32[1024,2304]{1,0:T(8,128)} %get-tuple-element.89) | data formatting | bytes 18874368 | tf_op jit(solution)/shard_map/reshape | solution.py:75
  36.1 8.0 fusion.15
  44.2 0.7 all-gather.7.cloned.1.call-update
  45.0 0.1 all_gather.30
  45.1 5.3 select_reduce_fusion
  50.4 0.1 all_gather.32
  50.6 6.2 all_gather.33
  56.9 5.6 all_gather.31
  62.5 7.2 all-gather.15.cloned.1.call-done
  69.7 1.1 slice.40
  70.8 0.3 copy.48
  71.1 1.1 slice-done
  72.2 4.9 while.14
  72.2 0.1 copy.105
  72.4 0.1 copy.106
  72.5 1.3 fusion.75
  73.9 0.1 copy.105
  74.0 0.2 copy.106
  74.2 1.3 fusion.75
  75.5 0.1 copy.105
  75.7 0.1 copy.106
  75.9 1.3 fusion.75
  77.2 0.1 copy.50
  77.3 0.1 fusion.55
  77.5 16.4 %all-gather.7.cloned.1.call-done = bf16[512,2048]{1,0:T(8,128)(2,1)} async-done(((bf16[512,512]{1,0:T(8,128)(2,1)}), bf16[512,2048]{1,0:T(8,128)(2,1)}) %all-gather.7.cloned.1.call-update) | async-done | bytes 2097168 | tf_op jit(solution)/shard_map/all_gather | solution.py:94
  93.9 2.1 fusion.59
  96.0 0.8 copy-done.2
  96.9 0.5 all-gather.9.cloned.1.call-update
  97.5 0.5 all-gather.11.cloned.1.call-update
  98.1 0.5 all-gather.13.cloned.1.call-update
  98.8 0.1 eq.33
  98.9 0.1 eq.29
  99.1 0.9 reduce-window.6
  100.0 0.2 slice_reduce_fusion
  100.4 0.1 mul.102
  100.5 0.1 fusion.57
  100.7 34.6 %all-reduce.2.cloned.1.call-done = f32[64,2048]{1,0:T(8,128)} async-done(((f32[64,2048]{1,0:T(8,128)}), f32[64,2048]{1,0:T(8,128)}) %all-reduce.2.cloned.1.call-update) | async-done | bytes 524304 | tf_op jit(solution)/shard_map/psum | solution.py:101
  135.3 1.2 multiply_reduce_fusion.1
  136.5 1.2 multiply_convert_fusion
  137.7 9.7 scatter_custom_fusion
  147.3 28.3 %all_to_all.15 = bf16[2,32,8,2048]{3,2,1,0:T(8,128)(2,1)S(1)} all-to-all(bf16[2,32,8,2048]{3,2,1,0:T(8,128)(2,1)} %bitcast.110), channel_id=1, replica_groups=mesh['req'=2,'ctx'=4,'tp'=4] {'req'}, dimensions={0} | all-to-all | bytes 4194304 | tf_op jit(solution)/shard_map/all_to_all | solution.py:123
  175.6 234.7 %all-gather.9.cloned.1.call-done = bf16[32,2048,352]{1,2,0:T(8,128)(2,1)} async-done(((bf16[32,512,352]{1,2,0:T(8,128)(2,1)}), bf16[32,2048,352]{1,2,0:T(8,128)(2,1)}) %all-gather.9.cloned.1.call-update) | async-done | bytes 46137360 | tf_op jit(solution)/shard_map/all_gather | solution.py:105
  410.4 24.8 %fusion.28 = f32[2,32,8,352]{3,2,0,1:T(8,128)S(1)} fusion(bf16[32,2048,352]{1,2,0:T(8,128)(2,1)} %all-gather.9.cloned.1.call-done, bf16[2,32,8,2048]{3,2,1,0:T(8,128)(2,1)S(1)} %all_to_all.15), kind=kOutput, calls=%fused_computation.39 | convolution fusion | flops 738197504 | bytes 48955392 | tf_op jit(solution)/shard_map/resd,edf->resf/dot_general | solution.py:124
  435.1 250.3 %all-gather.11.cloned.1.call-done = bf16[32,2048,352]{1,2,0:T(8,128)(2,1)} async-done(((bf16[32,512,352]{1,2,0:T(8,128)(2,1)}), bf16[32,2048,352]{1,2,0:T(8,128)(2,1)}) %all-gather.11.cloned.1.call-update) | async-done | bytes 46137360 | tf_op jit(solution)/shard_map/all_gather | solution.py:106
  685.4 25.0 %fusion.43 = bf16[2,32,8,352]{3,2,0,1:T(8,128)(2,1)S(1)} fusion(bf16[32,2048,352]{1,2,0:T(8,128)(2,1)} %all-gather.11.cloned.1.call-done, bf16[2,32,8,2048]{3,2,1,0:T(8,128)(2,1)S(1)} %all_to_all.15, f32[2,32,8,352]{3,2,0,1:T(8,128)S(1)} %fusion.28), kind=kOutput, calls=%fused_computation.42 | convolution fusion | flops 739278848 | bytes 49315840 | tf_op jit(solution)/shard_map/resd,edf->resf/dot_general | solution.py:125
  710.5 250.0 %all-gather.13.cloned.1.call-done = bf16[32,352,2048]{2,1,0:T(8,128)(2,1)} async-done(((bf16[32,352,512]{2,1,0:T(8,128)(2,1)}), bf16[32,352,2048]{2,1,0:T(8,128)(2,1)}) %all-gather.13.cloned.1.call-update) | async-done | bytes 46137360 | tf_op jit(solution)/shard_map/all_gather | solution.py:107
  960.5 17.5 %fusion.21 = bf16[2,32,8,2048]{3,2,0,1:T(8,128)(2,1)S(1)} fusion(bf16[2,32,8,352]{3,2,0,1:T(8,128)(2,1)S(1)} %fusion.43, bf16[32,352,2048]{2,1,0:T(8,128)(2,1)} %all-gather.13.cloned.1.call-done), kind=kOutput, calls=%fused_computation.32 | convolution fusion | flops 739246080 | bytes 48594944 | tf_op jit(solution)/shard_map/resf,efd->resd/dot_general | solution.py:127
  978.0 0.1 copy.57
  978.1 28.1 %all_to_all.16 = bf16[2,32,8,2048]{3,2,1,0:T(8,128)(2,1)S(1)} all-to-all(bf16[2,32,8,2048]{3,2,1,0:T(8,128)(2,1)S(1)} %copy.57), channel_id=1, replica_groups=mesh['req'=2,'ctx'=4,'tp'=4] {'req'}, dimensions={0} | all-to-all | bytes 4194304 | tf_op jit(solution)/shard_map/all_to_all | solution.py:130
  1006.2 0.2 slice_bitcast_fusion.3
  1006.4 1.6 pad_maximum_fusion
  1008.0 4.7 all-to-all-start.2
  1012.8 47.7 %all-to-all-done.2 = bf16[4,2,32,8,512]{4,3,2,1,0:T(8,128)(2,1)S(1)} async-done(((bf16[4,2,32,8,512]{4,3,2,1,0:T(8,128)(2,1)}), bf16[4,2,32,8,512]{4,3,2,1,0:T(8,128)(2,1)S(1)}, u32[]{:S(2)}, u32[]{:S(2)}) %all-to-all-start.2) | async-done | bytes 2097184 | tf_op jit(solution)/shard_map/all_to_all | solution.py:14
  1060.5 0.3 convert_reduce_fusion
  1060.9 1.6 gather_fusion
  1062.6 0.4 multiply_reduce_fusion
  1063.0 1.6 add_convert_fusion
  (55 shorter events, 1.4 us)
Async XLA Ops:
  6.5 11.3 %copy-start = (bf16[256,4,128]{2,1,0:T(4,128)(2,1)S(1)}, bf16[256,4,128]{2,1,0:T(4,128)(2,1)}, u32[]{:S(2)}) copy-start(bf16[256,4,128]{2,1,0:T(4,128)(2,1)} %param.16) | copy-start | bytes 786436
  6.5 63.2 %all-gather.15.cloned.1.call-start = ((), (), s32[]{:S(2)}) async-start(), calls=%async_computation.8 | async-start | bytes 2621440 | tf_op jit(solution)/shard_map/all_gather | solution.py:19
  12.2 5.6 copy-start.3
  24.7 11.4 %copy-start.8 = (bf16[256,1,128]{2,0,1:T(8,128)(2,1)S(1)}, bf16[256,1,128]{2,0,1:T(8,128)(2,1)}, u32[]{:S(2)}) copy-start(bf16[256,1,128]{2,0,1:T(8,128)(2,1)} %param.18) | copy-start | bytes 196612
  44.2 49.8 %all-gather.7.cloned.1.call-start = ((), (), s32[]{:S(2)}) async-start(), calls=%async_computation.3 | async-start | bytes 2621440 | tf_op jit(solution)/shard_map/all_gather | solution.py:94
  44.9 90.4 %all-reduce.2.cloned.1.call-start = ((), (), s32[]{:S(2)}) async-start(), calls=%async_computation.4 | async-start | bytes 1048576 | tf_op jit(solution)/shard_map/psum | solution.py:101
  70.8 1.4 slice-start
  77.1 18.8 %copy-start.4 = (bf16[64,512]{1,0:T(8,128)(2,1)S(1)}, bf16[64,512]{1,0:T(8,128)(2,1)}, u32[]{:S(2)}) copy-start(bf16[64,512]{1,0:T(8,128)(2,1)} %param.22) | copy-start | bytes 196612
  96.0 0.8 copy-start.2
  96.8 313.5 %all-gather.9.cloned.1.call-start = ((), (), s32[]{:S(2)}) async-start(), calls=%async_computation.5 | async-start | bytes 57671680 | tf_op jit(solution)/shard_map/all_gather | solution.py:105
  97.4 588.0 %all-gather.11.cloned.1.call-start = ((), (), s32[]{:S(2)}) async-start(), calls=%async_computation.6 | async-start | bytes 57671680 | tf_op jit(solution)/shard_map/all_gather | solution.py:106
  98.0 0.7 copy-start.5
  98.0 38.5 %copy-start.6 = (f32[2048]{0:T(1024)S(1)}, f32[2048]{0:T(1024)}, u32[]{:S(2)}) copy-start(f32[2048]{0:T(1024)} %param.24) | copy-start | bytes 24580
  98.0 862.5 %all-gather.13.cloned.1.call-start = ((), (), s32[]{:S(2)}) async-start(), calls=%async_computation.7 | async-start | bytes 57671680 | tf_op jit(solution)/shard_map/all_gather | solution.py:107
  1008.0 4.7 copy-start.7
  1008.0 52.5 %all-to-all-start.2 = ((bf16[4,2,32,8,512]{4,3,2,1,0:T(8,128)(2,1)}), bf16[4,2,32,8,512]{4,3,2,1,0:T(8,128)(2,1)S(1)}, u32[]{:S(2)}, u32[]{:S(2)}) async-start(bf16[4,2,32,8,512]{4,3,2,1,0:T(8,128)(2,1)} %pad_maximum_fusion), calls=%async_computation.2 | async-start | bytes 4194304 | tf_op jit(solution)/shard_map/all_to_all | solution.py:14
  1060.9 3.7 copy-start.1
Sparse Core Ops, SparseCore 0:
  44.3 25.3 all-gather.14
  71.3 22.6 all-gather.6
  97.0 38.2 all-reduce.1
  136.7 273.5 all-gather.8
  411.8 273.5 all-gather.10
  686.9 273.5 all-gather.12
